TPU v7x, 32 devices: a whole 2x2x4 slice. The times are simulated.
32 devices in a mesh: section: 2 (over x), bits: 4 (over z), rep: 4 (over y, core).
Axes of the slice: x: 2, y: 2, z: 4, core: 2. Of those that a mesh axis runs over, the one named last changes fastest.
Arguments:
- left_stems: bfloat16 [8, 1024, 2, 4, 256], P('rep', 'section', None, 'bits'), may hold values from -6 to 6
- right_stems: bfloat16 [8, 1024, 2, 256], P('rep', 'section'), may hold values from -6 to 6
- left_gate: bfloat16 [2, 256, 256], replicated, may hold values from -0.25 to 0.25
- mix_gate: bfloat16 [2, 256, 256], replicated, may hold values from -0.25 to 0.25
- right_gate: bfloat16 [2, 256, 256], replicated, may hold values from -0.25 to 0.25
- left_low: int32 [4096], P('bits'), may hold values from 0 to 255
- right_index: int32 [4096], P('bits'), may hold values from 0 to 255
Outputs:
- amplitudes: float32 [2, 4096], P(None, 'bits')
Inputs may be any that keep to these rules, and one draw needn't show every extreme that they name: Bitstring t has left index (t // 1024) * 256 + left_low[t].
All inputs are finite; a program needn't handle non-finite values.
Results may differ from a plain program's by a relative error of at most 0.015.
Values may be sent and summed in bfloat16 or wider, within the bound.
A program may use at most 128 MiB of HBM per device.

v0:
```python
import math

import jax
import jax.numpy as jnp
from jax import lax
from jax.sharding import PartitionSpec as P


def complex_matrix(gate):
    real_part = gate[0]
    imag_part = gate[1]
    upper_half = jnp.concatenate([real_part, imag_part], axis=1)
    bottom = jnp.concatenate([-imag_part, real_part], axis=1)
    return jnp.concatenate([upper_half, bottom], axis=0)


def body(left_stems, right_stems, left_gate, mix_gate, right_gate, left_low, right_index):
    width = left_gate.shape[1]
    groups = lax.axis_size("bits")
    low_width = width // groups
    row_count = left_stems.shape[0] * left_stems.shape[1]
    first_matrix = complex_matrix(left_gate)
    right_matrix = complex_matrix(right_gate)
    stem_rows = left_stems.reshape(row_count, 2 * width)
    first_pass = jnp.dot(stem_rows, first_matrix, preferred_element_type=jnp.float32).astype(
        jnp.bfloat16
    )
    right_rows_all = right_stems.reshape(row_count, 2 * width)
    right_final = jnp.dot(right_rows_all, right_matrix, preferred_element_type=jnp.float32).astype(
        jnp.bfloat16
    )
    right_final = right_final.reshape(row_count, 2, width)
    total_terms = (
        left_stems.shape[0] * lax.axis_size("rep") * left_stems.shape[1] * lax.axis_size("section")
    )
    norm_factor = 1.0 / math.sqrt(total_terms)
    first_rows = first_pass.reshape(row_count, 2, width)
    pairs = lax.dot_general(
        first_rows, right_final, (((0,), (0,)), ((), ())), preferred_element_type=jnp.float32
    )
    block_real = pairs[0, :, 0, :] - pairs[1, :, 1, :]
    block_imag = pairs[0, :, 1, :] + pairs[1, :, 0, :]
    blocks = jnp.stack([block_real, block_imag]).reshape(2, groups, low_width, width)
    received = lax.all_to_all(
        blocks.astype(jnp.bfloat16), "bits", split_axis=1, concat_axis=1, tiled=True
    ).astype(blocks.dtype)
    received = received.reshape(2, width, width)
    mix_columns = mix_gate[:, :, left_low].astype(jnp.float32)
    sum_columns = received[:, :, right_index]
    amp_real = jnp.sum(mix_columns[0] * sum_columns[0] - mix_columns[1] * sum_columns[1], axis=0)
    amp_imag = jnp.sum(mix_columns[0] * sum_columns[1] + mix_columns[1] * sum_columns[0], axis=0)
    partial_value = jnp.stack([amp_real, amp_imag])
    picked = lax.psum(partial_value, ("section", "rep"))
    return picked * norm_factor


def solution(mesh):
    in_specs = (
        P("rep", "section", None, "bits", None),
        P("rep", "section", None, None),
        P(),
        P(),
        P(),
        P("bits"),
        P("bits"),
    )
    out_specs = P(None, "bits")
    return jax.shard_map(body, mesh=mesh, in_specs=in_specs, out_specs=out_specs, check_vma=False)
```

profile of v0, /device:TPU:0, one launch (start us, length us, event | category | flops | bytes accessed | tf_op | source)
XLA Modules:
  0.0 50.2 jit_solution(15778732135810141312)
XLA Ops:
  0.0 0.0 copy-start
  0.0 0.0 copy-start.1
  0.0 1.1 %slice_bitcast_fusion = (bf16[256,256]{1,0:T(8,128)(2,1)S(1)}, bf16[256,256]{1,0:T(8,128)(2,1)S(1)}) fusion(bf16[2,256,256]{2,1,0:T(8,128)(2,1)} %param.11), kind=kLoop, calls=%fused_computation.27 | loop fusion | bytes 524288 | tf_op jit(solution)/shard_map/squeeze | solution.py:11
  1.1 0.9 %fusion.21 = bf16[256,256]{1,0:T(8,128)(2,1)S(1)} fusion(bf16[2,256,256]{2,1,0:T(8,128)(2,1)} %param.11), kind=kLoop, calls=%fused_computation.40 | loop fusion | flops 65536 | bytes 262144 | tf_op jit(solution)/shard_map/neg | solution.py:13
  2.1 1.0 %slice_bitcast_fusion.2 = (bf16[256,256]{1,0:T(8,128)(2,1)S(1)}, bf16[256,256]{1,0:T(8,128)(2,1)S(1)}) fusion(bf16[2,256,256]{2,1,0:T(8,128)(2,1)} %param.9), kind=kLoop, calls=%fused_computation.29 | loop fusion | bytes 524288 | tf_op jit(solution)/shard_map/squeeze | solution.py:11
  3.1 0.9 %fusion.20 = bf16[256,256]{1,0:T(8,128)(2,1)S(1)} fusion(bf16[2,256,256]{2,1,0:T(8,128)(2,1)} %param.9), kind=kLoop, calls=%fused_computation.39 | loop fusion | flops 65536 | bytes 262144 | tf_op jit(solution)/shard_map/neg | solution.py:13
  4.0 0.0 copy-done
  4.0 0.2 copy.25
  4.2 0.0 copy-done.1
  4.2 0.2 copy.24
  4.5 0.8 %convolution_convert_fusion = bf16[512,1024]{1,0:T(8,128)(2,1)S(1)} fusion(bf16[1024,512]{1,0:T(8,128)(2,1)S(1)} %bitcast.53, bf16[256,256]{1,0:T(8,128)(2,1)S(1)} %get-tuple-element.10, bf16[256,256]{1,0:T(8,128)(2,1)S(1)} %fusion.21, bf16[256,256]{1,0:T(8,128)(2,1)S(1)} %get-tuple-element.9), kind=kOutput, calls=%fused_computation.3 | convolution fusion | flops 539492352 | bytes 2490368 | tf_op jit(solution)/shard_map/dot_general | solution.py:29
  5.2 0.8 %convolution_convert_fusion.1 = bf16[512,1024]{1,0:T(8,128)(2,1)S(1)} fusion(bf16[1024,512]{1,0:T(8,128)(2,1)S(1)} %bitcast.52, bf16[256,256]{1,0:T(8,128)(2,1)S(1)} %get-tuple-element.12, bf16[256,256]{1,0:T(8,128)(2,1)S(1)} %fusion.20, bf16[256,256]{1,0:T(8,128)(2,1)S(1)} %get-tuple-element.11), kind=kOutput, calls=%fused_computation.4 | convolution fusion | flops 539492352 | bytes 2490368 | tf_op jit(solution)/shard_map/dot_general | solution.py:25
  6.0 0.0 copy-start.3
  6.0 0.0 copy-start.4
  6.0 0.0 copy-start.2
  6.0 0.7 %fusion.22 = f32[2,256,2,256]{3,1,2,0:T(8,128)S(1)} fusion(bf16[1024,2,256,1]{0,2,3,1:T(8,128)(2,1)S(1)} %bitcast.59, bf16[1024,2,256,1]{0,2,1,3:T(8,128)(2,1)S(1)} %bitcast.58), kind=kOutput, calls=%fused_computation.41 | convolution fusion | flops 536870912 | bytes 3145728 | tf_op jit(solution)/shard_map/dot_general | solution.py:38
  6.8 0.1 fusion.15
  6.8 0.7 %pad_maximum_fusion = bf16[2,4,64,256]{3,2,0,1:T(8,128)(2,1)} fusion(bf16[1,4,64,256]{3,2,0,1:T(8,128)(2,1)S(1)} %bitcast.55, bf16[1,4,64,256]{3,2,0,1:T(8,128)(2,1)S(1)} %bitcast.54), kind=kLoop, calls=%fused_computation.25 | loop fusion | flops 131072 | bytes 524288 | tf_op jit(solution)/shard_map/stack | solution.py:43
  7.6 6.3 %all-to-all-start = ((bf16[2,4,64,256]{3,2,0,1:T(8,128)(2,1)}), bf16[2,4,64,256]{3,2,0,1:T(8,128)(2,1)S(1)}, u32[]{:S(2)}, u32[]{:S(2)}) async-start(bf16[2,4,64,256]{3,2,0,1:T(8,128)(2,1)} %pad_maximum_fusion), calls=%async_computation | async-start | bytes 524288 | tf_op jit(solution)/shard_map/all_to_all | solution.py:44
  13.9 0.0 copy-done.3
  13.9 0.0 copy-done.4
  14.0 0.0 copy-done.2
  14.0 0.2 copy.15
  14.2 4.2 %gather_fusion = bf16[1024,2,256]{2,1,0:T(2,128)(2,1)S(1)} fusion(bf16[2,256,256]{1,0,2:T(2,128)(2,1)S(1)} %copy.15, s32[1024]{0:T(1024)S(1)} %fusion.16), kind=kCustom, calls=%fused_computation | custom fusion | bytes 2101248 | tf_op jit(solution)/shard_map/gather | solution.py:48
  18.3 2.1 %convert_bitcast_fusion = f32[2,256,1024]{1,0,2:T(2,128)} fusion(bf16[1024,2,256]{2,1,0:T(2,128)(2,1)S(1)} %gather_fusion), kind=kLoop, calls=%fused_computation.2 | loop fusion | flops 524288 | bytes 3145728 | tf_op jit(solution)/shard_map/convert_element_type | solution.py:48
  20.4 2.5 %all-to-all-done = bf16[2,4,64,256]{3,2,0,1:T(8,128)(2,1)S(1)} async-done(((bf16[2,4,64,256]{3,2,0,1:T(8,128)(2,1)}), bf16[2,4,64,256]{3,2,0,1:T(8,128)(2,1)S(1)}, u32[]{:S(2)}, u32[]{:S(2)}) %all-to-all-start) | async-done | bytes 262176 | tf_op jit(solution)/shard_map/all_to_all | solution.py:44
  22.9 0.1 bitcast_convert_fusion
  22.9 0.2 copy.20
  23.2 4.1 %gather_fusion.1 = f32[1024,2,256]{2,1,0:T(2,128)S(1)} fusion(f32[2,256,256]{1,0,2:T(2,128)S(1)} %copy.20, s32[1024]{0:T(1024)S(1)} %fusion.17), kind=kCustom, calls=%fused_computation.1 | custom fusion | bytes 4198400 | tf_op jit(solution)/shard_map/gather | solution.py:49
  27.3 9.9 %subtract_reduce_fusion = (f32[1024]{0:T(1024)S(1)}, f32[1024]{0:T(1024)S(1)}) fusion(f32[2,256,1024]{1,0,2:T(2,128)S(1)} %bitcast.49, f32[2,256,1024]{1,0,2:T(2,128)} %convert_bitcast_fusion), kind=kLoop, calls=%fused_computation.6 | loop fusion | flops 2095104 | bytes 4202496 | tf_op jit(solution)/shard_map/reduce_sum | solution.py:50
  37.2 12.3 %psum.7 = f32[2,1024]{1,0:T(2,128)S(1)} all-reduce(f32[2,1024]{1,0:T(2,128)S(1)} %pad_maximum_fusion.1), channel_id=1, replica_groups=mesh['section'=2,'bits'=4,'rep'=4] {'section','rep'}, use_global_device_ids=true, to_apply=%region_2.0 | all-reduce | flops 2048 | bytes 16384 | tf_op jit(solution)/shard_map/psum | solution.py:53
  49.5 0.6 %broadcast_multiply_fusion = f32[2,1024]{1,0:T(2,128)} fusion(f32[2,1024]{1,0:T(2,128)S(1)} %psum.7), kind=kLoop, calls=%fused_computation.36 | loop fusion | flops 2048 | bytes 16384 | tf_op jit(solution)/shard_map/mul | solution.py:54
  (4 shorter events, 0.0 us)
Async XLA Ops:
  0.0 4.0 %copy-start = (bf16[2,512,2,256]{3,2,1,0:T(2,128)(2,1)S(1)}, bf16[2,512,2,256]{3,2,1,0:T(2,128)(2,1)}, u32[]{:S(2)}) copy-start(bf16[2,512,2,256]{3,2,1,0:T(2,128)(2,1)} %param.8) | copy-start | bytes 3145732
  0.0 4.2 %copy-start.1 = (bf16[2,512,2,1,256]{4,2,3,1,0:T(2,128)(2,1)S(1)}, bf16[2,512,2,1,256]{4,2,3,1,0:T(2,128)(2,1)}, u32[]{:S(2)}) copy-start(bf16[2,512,2,1,256]{4,2,3,1,0:T(2,128)(2,1)} %param.7) | copy-start | bytes 3145732
  6.0 7.9 %copy-start.3 = (s32[1024]{0:T(1024)S(1)}, s32[1024]{0:T(1024)}, u32[]{:S(2)}) copy-start(s32[1024]{0:T(1024)} %param.13) | copy-start | bytes 12292
  6.0 7.9 %copy-start.4 = (s32[1024]{0:T(1024)S(1)}, s32[1024]{0:T(1024)}, u32[]{:S(2)}) copy-start(s32[1024]{0:T(1024)} %param.12) | copy-start | bytes 12292
  6.0 8.0 %copy-start.2 = (bf16[2,256,256]{2,1,0:T(8,128)(2,1)S(1)}, bf16[2,256,256]{2,1,0:T(8,128)(2,1)}, u32[]{:S(2)}) copy-start(bf16[2,256,256]{2,1,0:T(8,128)(2,1)} %param.10) | copy-start | bytes 786436
  7.6 15.3 %all-to-all-start = ((bf16[2,4,64,256]{3,2,0,1:T(8,128)(2,1)}), bf16[2,4,64,256]{3,2,0,1:T(8,128)(2,1)S(1)}, u32[]{:S(2)}, u32[]{:S(2)}) async-start(bf16[2,4,64,256]{3,2,0,1:T(8,128)(2,1)} %pad_maximum_fusion), calls=%async_computation | async-start | bytes 524288 | tf_op jit(solution)/shard_map/all_to_all | solution.py:44
where the time goes:
time: 50.4 us; the launch traced here: 50.2 us
  other arithmetic  15.3 us (30%)
  blocking collectives  12.3 us (24%)
  local copies, waits for them, and re-layouts  11.3 us (22%)
  starting transfers between devices  6.34 us (13%)
  waiting for transfers between devices  2.45 us (5%)
  matrix products  2.25 us (4%)
    psum x1, blocking collectives, body(): picked = lax.psum(partial_value, ('section', 'rep'))  12.3 us
    reduce_sum x1, other arithmetic, body(): jnp.sum(mix_columns[0] * sum_columns[0] - mix_columns[1] * sum_columns[1]...  9.9 us
    all_to_all x1, starting transfers between devices, body(): lax.all_to_all(blocks.astype(jnp.bfloat16), 'bits', split_axis=1, concat_...  6.34 us
    gather x1, local copies, waits for them, and re-layouts, body(): mix_columns = mix_gate[:, :, left_low].astype(jnp.float32)  4.17 us
    gather x1, local copies, waits for them, and re-layouts, body(): sum_columns = received[:, :, right_index]  4.14 us
    all_to_all x1, waiting for transfers between devices, body(): lax.all_to_all(blocks.astype(jnp.bfloat16), 'bits', split_axis=1, concat_...  2.45 us
    squeeze x2, local copies, waits for them, and re-layouts, complex_matrix(): imag_part = gate[1]  2.12 us
    convert_element_type x1, other arithmetic, body(): mix_columns = mix_gate[:, :, left_low].astype(jnp.float32)  2.06 us
  transfers between devices with their start and end apart: 1, of which 1 were waited for; matrix products, arithmetic and copies ran while one was open for 13% of the time, Pallas kernels for 0%

commit v1 on v0

v1 whole, which is shorter than its diff:
```python
import functools
import math

import jax
import jax.numpy as jnp
from jax import lax
from jax.experimental import pallas as pl
from jax.experimental.pallas import tpu as pltpu
from jax.sharding import PartitionSpec as P

MESH = pl.DeviceIdType.MESH
CHUNKS = 4


def flip(index, mask, size):
    total, place = 0, 1
    while place < size:
        bit = lax.rem(index // place, 2)
        total = total + (1 - bit if (mask // place) % 2 else bit) * place
        place *= 2
    return total


def dot(a, b):
    return jnp.dot(a, b, preferred_element_type=jnp.float32)


def dot_t(a, b):
    return lax.dot_general(a, b, (((0,), (0,)), ((), ())), preferred_element_type=jnp.float32)


def onehot(index_rows, width):
    lanes = index_rows.shape[1]
    spots = lax.broadcasted_iota(jnp.int32, (width, lanes), 0)
    parts = [
        jnp.where(spots == index_rows[s : s + 1, :], 1.0, 0.0).astype(jnp.bfloat16)
        for s in range(index_rows.shape[0])
    ]
    return jnp.concatenate(parts, axis=1)


def kernel(
    sizes, norm,
    left_hbm, right_hbm, left_gate_hbm, mix_hbm, right_gate_hbm, low_ref, right_index_ref,
    out_ref,
    left_buf, right_buf, left_gate, mix_rows, right_gate, u_ref,
    idx_buf, z_send, z_recv, plane,
    load_sem, gate_sem, idx_send_sem, idx_recv_sem, z_send_sem, z_recv_sem, p_send_sem, p_recv_sem,
):
    groups, sections, reps = sizes
    me, sec, rep = lax.axis_index("bits"), lax.axis_index("section"), lax.axis_index("rep")
    width = left_gate.shape[1]
    low_width = width // groups
    z_peers = [(x, {"bits": flip(me, x, groups)}) for x in range(1, groups)]
    plane_peers = []
    for a in range(sections):
        for b in range(reps):
            if a or b:
                s, r = flip(sec, a, sections), flip(rep, b, reps)
                plane_peers.append((s * reps + r, {"section": s, "rep": r}, a * reps + b))

    barrier = pltpu.get_barrier_semaphore()
    for _, peer in z_peers:
        pl.semaphore_signal(barrier, inc=1, device_id=peer, device_id_type=MESH)
    for _, peer, _ in plane_peers:
        pl.semaphore_signal(barrier, inc=1, device_id=peer, device_id_type=MESH)

    rows = left_buf.shape[0]
    step = rows // CHUNKS
    left_rows, right_rows = left_hbm.reshape(rows, width), right_hbm.reshape(rows, width)
    loads = []
    for c in range(CHUNKS):
        at = pl.ds(c * step, step)
        pair = (
            pltpu.make_async_copy(right_rows.at[at], right_buf.at[at], load_sem.at[0, c]),
            pltpu.make_async_copy(left_rows.at[at], left_buf.at[at], load_sem.at[1, c]),
        )
        for copy in pair:
            copy.start()
        loads.append(pair)
    mine = pl.ds(pl.multiple_of(me * low_width, low_width), low_width)
    gate_loads = [
        pltpu.make_async_copy(left_gate_hbm, left_gate, gate_sem.at[0]),
        pltpu.make_async_copy(right_gate_hbm, right_gate, gate_sem.at[1]),
        pltpu.make_async_copy(mix_hbm.at[:, mine, :], mix_rows, gate_sem.at[2]),
    ]
    for copy in gate_loads:
        copy.start()

    block = min(width, step)
    row_at = lax.broadcasted_iota(jnp.int32, (block, block), 0)
    column_at = lax.broadcasted_iota(jnp.int32, (block, block), 1)
    swap = jnp.where(row_at + 1 - 2 * lax.rem(row_at, 2) == column_at, 1.0, 0.0).astype(jnp.bfloat16)
    parity = lax.rem(lax.broadcasted_iota(jnp.int32, (block, width), 0), 2)
    sign = (1 - 2 * parity).astype(jnp.float32).astype(jnp.bfloat16)
    total = jnp.zeros((width, 2 * width), jnp.float32)
    for c in range(CHUNKS):
        for copy in loads[c]:
            copy.wait()
        pieces = []
        for b in range(step // block):
            at = pl.ds(c * step + b * block, block)
            r = right_buf[at, :]
            pieces.append(jnp.concatenate([r * sign, dot(swap, r).astype(jnp.bfloat16)], axis=1))
        total = total + dot_t(left_buf[pl.ds(c * step, step), :], jnp.concatenate(pieces, axis=0))
    q = total.astype(jnp.bfloat16)

    pl.semaphore_wait(barrier, len(z_peers) + len(plane_peers))
    idx_copies = []
    for x, peer in z_peers:
        for w, ref in enumerate((low_ref, right_index_ref)):
            copy = pltpu.make_async_remote_copy(
                src_ref=ref, dst_ref=idx_buf.at[x, w],
                send_sem=idx_send_sem.at[x, w], recv_sem=idx_recv_sem.at[x, w],
                device_id=peer, device_id_type=MESH,
            )
            copy.start()
            idx_copies.append(copy)

    for copy in gate_loads:
        copy.wait()
    g0, g1 = dot_t(left_gate[0], q), dot_t(left_gate[1], q)
    t_real = (g0[:, :width] - g1[:, width:]).astype(jnp.bfloat16)
    t_imag = (g0[:, width:] + g1[:, :width]).astype(jnp.bfloat16)
    t = jnp.concatenate([t_real, t_imag], axis=0)
    h0, h1 = dot(t, right_gate[0]), dot(t, right_gate[1])
    u_ref[0] = h0[:width] - h1[width:]
    u_ref[1] = h0[width:] + h1[:width]
    mix = jnp.concatenate([mix_rows[0], mix_rows[1]], axis=0)

    def amplitudes(j, low, right, write):
        at = pl.ds(pl.multiple_of(j * low_width, low_width), low_width)
        u = jnp.concatenate([u_ref[0, at, :], u_ref[1, at, :]], axis=0).astype(jnp.bfloat16)
        index_rows, lanes = low.shape
        part = 2 if index_rows % 2 == 0 else 1
        for k in range(0, index_rows, part):
            x = dot(mix, onehot(low[k : k + part], width))
            v = dot(u, onehot(right[k : k + part], width))
            x0, x1, v0, v1 = x[:low_width], x[low_width:], v[:low_width], v[low_width:]
            real = jnp.sum(x0 * v0 - x1 * v1, axis=0, keepdims=True)
            imag = jnp.sum(x0 * v1 + x1 * v0, axis=0, keepdims=True)
            write(pl.ds(k * lanes, part * lanes), real, imag)

    def write_to(ref, slot):
        def write(at, real, imag):
            ref[slot, 0:1, at] = real
            ref[slot, 1:2, at] = imag

        return write

    amplitudes(me, low_ref[...], right_index_ref[...], write_to(z_recv, 0))

    z_copies = []
    for n, (x, peer) in enumerate(z_peers):
        idx_copies[2 * n].wait_recv()
        idx_copies[2 * n + 1].wait_recv()
        amplitudes(peer["bits"], idx_buf[x, 0], idx_buf[x, 1], write_to(z_send, x))
        copy = pltpu.make_async_remote_copy(
            src_ref=z_send.at[x], dst_ref=z_recv.at[x],
            send_sem=z_send_sem.at[x], recv_sem=z_recv_sem.at[x],
            device_id=peer, device_id_type=MESH,
        )
        copy.start()
        z_copies.append(copy)

    own = z_recv[0]
    for x in range(1, groups):
        z_copies[x - 1].wait_recv()
        own = own + z_recv[x]
    here = sec * reps + rep
    plane[here] = own
    p_copies = []
    for there, peer, n in plane_peers:
        copy = pltpu.make_async_remote_copy(
            src_ref=plane.at[here], dst_ref=plane.at[here],
            send_sem=p_send_sem.at[n], recv_sem=p_recv_sem.at[n],
            device_id=peer, device_id_type=MESH,
        )
        copy.start()
        p_copies.append(copy)
    for copy in p_copies:
        copy.wait_recv()
    result = plane[0]
    for n in range(1, sections * reps):
        result = result + plane[n]
    out_ref[...] = result * norm
    for copy in idx_copies + z_copies + p_copies:
        copy.wait_send()


def body(left_stems, right_stems, left_gate, mix_gate, right_gate, left_low, right_index):
    width = left_gate.shape[1]
    sizes = tuple(lax.axis_size(name) for name in ("bits", "section", "rep"))
    groups, sections, reps = sizes
    pairs = left_stems.shape[0] * left_stems.shape[1]
    norm = 1.0 / math.sqrt(pairs * sections * reps)
    count = left_low.shape[0]
    index_shape = (count // 128, 128)
    bf16, f32 = jnp.bfloat16, jnp.float32
    hbm = pl.BlockSpec(memory_space=pltpu.HBM)
    vmem = pl.BlockSpec(memory_space=pltpu.VMEM)
    dma = pltpu.SemaphoreType.DMA
    return pl.pallas_call(
        functools.partial(kernel, sizes, norm),
        out_shape=jax.ShapeDtypeStruct((2, count), f32),
        in_specs=[hbm] * 5 + [vmem] * 2,
        out_specs=vmem,
        scratch_shapes=[
            pltpu.VMEM((2 * pairs, width), bf16),
            pltpu.VMEM((2 * pairs, width), bf16),
            pltpu.VMEM((2, width, width), bf16),
            pltpu.VMEM((2, width // groups, width), bf16),
            pltpu.VMEM((2, width, width), bf16),
            pltpu.VMEM((2, width, width), f32),
            pltpu.VMEM((groups, 2) + index_shape, jnp.int32),
            pltpu.VMEM((groups, 2, count), f32),
            pltpu.VMEM((groups, 2, count), f32),
            pltpu.VMEM((sections * reps, 2, count), f32),
            dma((2, CHUNKS)),
            dma((3,)),
            dma((groups, 2)),
            dma((groups, 2)),
            dma((groups,)),
            dma((groups,)),
            dma((sections * reps,)),
            dma((sections * reps,)),
        ],
        compiler_params=pltpu.CompilerParams(collective_id=0, has_side_effects=True),
        name="amplitudes",
    )(
        left_stems.reshape(pairs, 2, width), right_stems.reshape(pairs, 2, width),
        left_gate, mix_gate, right_gate,
        left_low.reshape(index_shape), right_index.reshape(index_shape),
    )


def solution(mesh):
    in_specs = (
        P("rep", "section", None, "bits", None),
        P("rep", "section", None, None),
        P(),
        P(),
        P(),
        P("bits"),
        P("bits"),
    )
    out_specs = P(None, "bits")
    return jax.shard_map(body, mesh=mesh, in_specs=in_specs, out_specs=out_specs, check_vma=False)
```

time: 50.4 us -> 20.2 us (0.40)
  Pallas kernels: 0 us -> 18.7 us
  other arithmetic: 15.3 us -> 0 us
  blocking collectives: 12.3 us -> 0 us
  local copies, waits for them, and re-layouts: 11.3 us -> 1.3 us
  starting transfers between devices: 6.34 us -> 0 us
  waiting for transfers between devices: 2.45 us -> 0 us
  matrix products: 2.25 us -> 0 us
    pallas_call x0 -> x1, Pallas kernels: none -> 18.7 us  [body(): pl.pallas_call(functools.partial(kernel, sizes, norm), out_shape=jax.Shap...]
    psum x1 -> x0, blocking collectives: 12.3 us -> none  [body(): picked = lax.psum(partial_value, ('section', 'rep'))]
    reduce_sum x1 -> x0, other arithmetic: 9.9 us -> none  [body(): jnp.sum(mix_columns[0] * sum_columns[0] - mix_columns[1] * sum_columns[1]...]
    gather x2 -> x0, local copies, waits for them, and re-layouts: 8.31 us -> none  [the longest x1 4.17 us: body(): mix_columns = mix_gate[:, :, left_low].astype(jnp.float32)]
    all_to_all x1 -> x0, starting transfers between devices: 6.34 us -> none  [body(): lax.all_to_all(blocks.astype(jnp.bfloat16), 'bits', split_axis=1, concat_...]
    all_to_all x1 -> x0, waiting for transfers between devices: 2.45 us -> none  [body(): lax.all_to_all(blocks.astype(jnp.bfloat16), 'bits', split_axis=1, concat_...]
    dot_general x3 -> x0, matrix products: 2.25 us -> none  [the longest x1 0.76 us: body(): jnp.dot(stem_rows, first_matrix, preferred_element_type=jnp.float32)]
    squeeze x2 -> x0, local copies, waits for them, and re-layouts: 2.12 us -> none  [complex_matrix(): imag_part = gate[1]]
  transfers between devices with their start and end apart: 1 -> 0, of which waited for: 1 -> 0; matrix products, arithmetic and copies ran while one was open for 13% -> 0% of each run, Pallas kernels for 0% -> 0%
where the time goes in v1:
time: 20.2 us; the launch traced here: 20 us
  Pallas kernels  18.7 us (93%)
  local copies, waits for them, and re-layouts  1.3 us (6%)
    pallas_call x1, Pallas kernels, body(): pl.pallas_call(functools.partial(kernel, sizes, norm), out_shape=jax.Shap...  18.7 us
    unnamed x1, local copies, waits for them, and re-layouts  1.3 us

profile of v1, /device:TPU:0, one launch (start us, length us, event | category | flops | bytes accessed | tf_op | source)
XLA Modules:
  0.0 20.0 jit_solution(13603932520940156036)
XLA Ops:
  0.0 18.7 %amplitudes.1 = f32[2,1024]{1,0:T(2,128)} custom-call(bf16[1024,2,256]{2,1,0:T(2,128)(2,1)} %bitcast.4, bf16[1024,2,256]{2,1,0:T(2,128)(2,1)} %bitcast.5, bf16[2,256,256]{2,1,0:T(8,128)(2,1)} %left_gate_hbm.1, bf16[2,256,256]{2,1,0:T(8,128)(2,1)} %mix_hbm.1, bf16[2,256,256]{2,1,0:T(8,128)(2,1)} %right_gate_hbm.1, s32[8,128]{1,0:T(8,128)} %bitcast.6, ...), custom_call_target="tpu_custom_call" | custom-call | tf_op jit(solution)/shard_map/amplitudes/pallas_call | solution.py:203
  18.7 1.3 %copy.9 = f32[2,1024]{1,0:T(2,128)} copy(f32[2,1024]{1,0:T(2,128)} %amplitudes.1) | data formatting | bytes 16384

commit v2 on v1

--- a/solution.py
+++ b/solution.py
@@ -41,10 +41,10 @@
 
 def kernel(
     sizes, norm,
-    left_hbm, right_hbm, left_gate_hbm, mix_hbm, right_gate_hbm, low_ref, right_index_ref,
+    left_hbm, right_hbm, left_gate_hbm, mix_hbm, right_gate_hbm, low_hbm, right_index_hbm,
     out_ref,
     left_buf, right_buf, left_gate, mix_rows, right_gate, u_ref,
-    idx_buf, z_send, z_recv, plane,
+    idx_buf, own_ref, z_send, z_recv, plane,
     load_sem, gate_sem, idx_send_sem, idx_recv_sem, z_send_sem, z_recv_sem, p_send_sem, p_recv_sem,
 ):
     groups, sections, reps = sizes
@@ -53,8 +53,8 @@
     low_width = width // groups
     z_peers = [(x, {"bits": flip(me, x, groups)}) for x in range(1, groups)]
     plane_peers = []
-    for a in range(sections):
-        for b in range(reps):
+    for a in reversed(range(sections)):
+        for b in reversed(range(reps)):
             if a or b:
                 s, r = flip(sec, a, sections), flip(rep, b, reps)
                 plane_peers.append((s * reps + r, {"section": s, "rep": r}, a * reps + b))
@@ -84,7 +84,11 @@
         pltpu.make_async_copy(right_gate_hbm, right_gate, gate_sem.at[1]),
         pltpu.make_async_copy(mix_hbm.at[:, mine, :], mix_rows, gate_sem.at[2]),
     ]
-    for copy in gate_loads:
+    idx_loads = [
+        pltpu.make_async_copy(low_hbm, idx_buf.at[0, 0], idx_recv_sem.at[0, 0]),
+        pltpu.make_async_copy(right_index_hbm, idx_buf.at[0, 1], idx_recv_sem.at[0, 1]),
+    ]
+    for copy in idx_loads + gate_loads:
         copy.start()
 
     block = min(width, step)
@@ -105,12 +109,14 @@
         total = total + dot_t(left_buf[pl.ds(c * step, step), :], jnp.concatenate(pieces, axis=0))
     q = total.astype(jnp.bfloat16)
 
+    for copy in idx_loads:
+        copy.wait()
     pl.semaphore_wait(barrier, len(z_peers) + len(plane_peers))
     idx_copies = []
     for x, peer in z_peers:
-        for w, ref in enumerate((low_ref, right_index_ref)):
+        for w in range(2):
             copy = pltpu.make_async_remote_copy(
-                src_ref=ref, dst_ref=idx_buf.at[x, w],
+                src_ref=idx_buf.at[0, w], dst_ref=idx_buf.at[x, w],
                 send_sem=idx_send_sem.at[x, w], recv_sem=idx_recv_sem.at[x, w],
                 device_id=peer, device_id_type=MESH,
             )
@@ -139,22 +145,22 @@
             x0, x1, v0, v1 = x[:low_width], x[low_width:], v[:low_width], v[low_width:]
             real = jnp.sum(x0 * v0 - x1 * v1, axis=0, keepdims=True)
             imag = jnp.sum(x0 * v1 + x1 * v0, axis=0, keepdims=True)
-            write(pl.ds(k * lanes, part * lanes), real, imag)
-
-    def write_to(ref, slot):
-        def write(at, real, imag):
-            ref[slot, 0:1, at] = real
-            ref[slot, 1:2, at] = imag
-
-        return write
-
-    amplitudes(me, low_ref[...], right_index_ref[...], write_to(z_recv, 0))
+            write(pl.ds(k * lanes, part * lanes), jnp.concatenate([real, imag], axis=0))
+
+    def write_own(at, value):
+        own_ref[:, at] = value
+
+    amplitudes(me, idx_buf[0, 0], idx_buf[0, 1], write_own)
 
     z_copies = []
     for n, (x, peer) in enumerate(z_peers):
         idx_copies[2 * n].wait_recv()
         idx_copies[2 * n + 1].wait_recv()
-        amplitudes(peer["bits"], idx_buf[x, 0], idx_buf[x, 1], write_to(z_send, x))
+
+        def write_send(at, value, x=x):
+            z_send[x, :, at] = value.astype(z_send.dtype)
+
+        amplitudes(peer["bits"], idx_buf[x, 0], idx_buf[x, 1], write_send)
         copy = pltpu.make_async_remote_copy(
             src_ref=z_send.at[x], dst_ref=z_recv.at[x],
             send_sem=z_send_sem.at[x], recv_sem=z_recv_sem.at[x],
@@ -163,12 +169,12 @@
         copy.start()
         z_copies.append(copy)
 
-    own = z_recv[0]
+    own = own_ref[...]
     for x in range(1, groups):
         z_copies[x - 1].wait_recv()
-        own = own + z_recv[x]
+        own = own + z_recv[x].astype(jnp.float32)
     here = sec * reps + rep
-    plane[here] = own
+    plane[here] = own.astype(plane.dtype)
     p_copies = []
     for there, peer, n in plane_peers:
         copy = pltpu.make_async_remote_copy(
@@ -180,9 +186,9 @@
         p_copies.append(copy)
     for copy in p_copies:
         copy.wait_recv()
-    result = plane[0]
+    result = plane[0].astype(jnp.float32)
     for n in range(1, sections * reps):
-        result = result + plane[n]
+        result = result + plane[n].astype(jnp.float32)
     out_ref[...] = result * norm
     for copy in idx_copies + z_copies + p_copies:
         copy.wait_send()
@@ -200,10 +206,11 @@
     hbm = pl.BlockSpec(memory_space=pltpu.HBM)
     vmem = pl.BlockSpec(memory_space=pltpu.VMEM)
     dma = pltpu.SemaphoreType.DMA
+    keep = functools.partial(pltpu.with_memory_space_constraint, memory_space=pltpu.HBM)
     return pl.pallas_call(
         functools.partial(kernel, sizes, norm),
         out_shape=jax.ShapeDtypeStruct((2, count), f32),
-        in_specs=[hbm] * 5 + [vmem] * 2,
+        in_specs=[hbm] * 7,
         out_specs=vmem,
         scratch_shapes=[
             pltpu.VMEM((2 * pairs, width), bf16),
@@ -213,9 +220,10 @@
             pltpu.VMEM((2, width, width), bf16),
             pltpu.VMEM((2, width, width), f32),
             pltpu.VMEM((groups, 2) + index_shape, jnp.int32),
-            pltpu.VMEM((groups, 2, count), f32),
-            pltpu.VMEM((groups, 2, count), f32),
-            pltpu.VMEM((sections * reps, 2, count), f32),
+            pltpu.VMEM((2, count), f32),
+            pltpu.VMEM((groups, 2, count), bf16),
+            pltpu.VMEM((groups, 2, count), bf16),
+            pltpu.VMEM((sections * reps, 2, count), bf16),
             dma((2, CHUNKS)),
             dma((3,)),
             dma((groups, 2)),
@@ -225,12 +233,14 @@
             dma((sections * reps,)),
             dma((sections * reps,)),
         ],
-        compiler_params=pltpu.CompilerParams(collective_id=0, has_side_effects=True),
+        compiler_params=pltpu.CompilerParams(
+            collective_id=0, has_side_effects=True, vmem_limit_bytes=16 * 1024 * 1024
+        ),
         name="amplitudes",
     )(
-        left_stems.reshape(pairs, 2, width), right_stems.reshape(pairs, 2, width),
-        left_gate, mix_gate, right_gate,
-        left_low.reshape(index_shape), right_index.reshape(index_shape),
+        keep(left_stems.reshape(pairs, 2, width)), keep(right_stems.reshape(pairs, 2, width)),
+        keep(left_gate), keep(mix_gate), keep(right_gate),
+        keep(left_low.reshape(index_shape)), keep(right_index.reshape(index_shape)),
     )
 
 

time: 20.2 us -> 18 us (0.89)
  Pallas kernels: 18.7 us -> 17.2 us
  local copies, waits for them, and re-layouts: 1.3 us -> 0.6 us
    pallas_call x1, Pallas kernels: 18.7 us -> 17.2 us  [body(): pl.pallas_call(functools.partial(kernel, sizes, norm), out_shape=jax.Shap...]
    unnamed x1, local copies, waits for them, and re-layouts: 1.3 us -> 0.6 us
where the time goes in v2:
time: 18 us; the launch traced here: 17.8 us
  Pallas kernels  17.2 us (96%)
  local copies, waits for them, and re-layouts  0.6 us (3%)
    pallas_call x1, Pallas kernels, body(): pl.pallas_call(functools.partial(kernel, sizes, norm), out_shape=jax.Shap...  17.2 us
    unnamed x1, local copies, waits for them, and re-layouts  0.6 us

profile of v2, /device:TPU:0, one launch (start us, length us, event | category | flops | bytes accessed | tf_op | source)
XLA Modules:
  0.0 17.8 jit_solution(11803313444174727735)
XLA Ops:
  0.0 17.2 %amplitudes.1 = f32[2,1024]{1,0:T(2,128)S(1)} custom-call(bf16[1024,2,256]{2,1,0:T(2,128)(2,1)} %bitcast.4, bf16[1024,2,256]{2,1,0:T(2,128)(2,1)} %bitcast.5, bf16[2,256,256]{2,1,0:T(8,128)(2,1)} %left_gate_hbm.1, bf16[2,256,256]{2,1,0:T(8,128)(2,1)} %mix_hbm.1, bf16[2,256,256]{2,1,0:T(8,128)(2,1)} %right_gate_hbm.1, s32[8,128]{1,0:T(8,128)} %bitcast.6, ...), custom_call_target="tpu_custom_call" | custom-call | tf_op jit(solution)/shard_map/amplitudes/pallas_call | solution.py:210
  17.2 0.6 %copy.9 = f32[2,1024]{1,0:T(2,128)} copy(f32[2,1024]{1,0:T(2,128)S(1)} %amplitudes.1) | data formatting | bytes 16384

commit v3 on v2

--- a/solution.py
+++ b/solution.py
@@ -43,15 +43,28 @@
     sizes, norm,
     left_hbm, right_hbm, left_gate_hbm, mix_hbm, right_gate_hbm, low_hbm, right_index_hbm,
     out_ref,
-    left_buf, right_buf, left_gate, mix_rows, right_gate, u_ref,
+    left_buf, right_buf, left_gate, mix_rows, right_gate, u_ref, mix_far, u_send, u_recv,
     idx_buf, own_ref, z_send, z_recv, plane,
-    load_sem, gate_sem, idx_send_sem, idx_recv_sem, z_send_sem, z_recv_sem, p_send_sem, p_recv_sem,
+    load_sem, gate_sem, idx_send_sem, idx_recv_sem, z_send_sem, z_recv_sem, p_send_sem, p_recv_sem, u_sem,
 ):
     groups, sections, reps = sizes
     me, sec, rep = lax.axis_index("bits"), lax.axis_index("section"), lax.axis_index("rep")
     width = left_gate.shape[1]
     low_width = width // groups
-    z_peers = [(x, {"bits": flip(me, x, groups)}) for x in range(1, groups)]
+    last = groups - 1
+    z_peers = [(x, {"bits": flip(me, x, groups)}) for x in [1, last] + list(range(2, last)) if x <= last]
+    if groups == 2:
+        z_peers = z_peers[:1]
+    far = jnp.logical_or(me == 0, me == last)
+    far_peer = {"bits": flip(me, last, groups)}
+    far_rows = pl.ds(pl.multiple_of(far_peer["bits"] * low_width, low_width), low_width)
+
+    def unless_far(x, run):
+        if x == last:
+            pl.when(jnp.logical_not(far))(run)
+        else:
+            run()
+
     plane_peers = []
     for a in reversed(range(sections)):
         for b in reversed(range(reps)):
@@ -83,6 +96,7 @@
         pltpu.make_async_copy(left_gate_hbm, left_gate, gate_sem.at[0]),
         pltpu.make_async_copy(right_gate_hbm, right_gate, gate_sem.at[1]),
         pltpu.make_async_copy(mix_hbm.at[:, mine, :], mix_rows, gate_sem.at[2]),
+        pltpu.make_async_copy(mix_hbm.at[:, far_rows, :], mix_far, gate_sem.at[3]),
     ]
     idx_loads = [
         pltpu.make_async_copy(low_hbm, idx_buf.at[0, 0], idx_recv_sem.at[0, 0]),
@@ -112,16 +126,37 @@
     for copy in idx_loads:
         copy.wait()
     pl.semaphore_wait(barrier, len(z_peers) + len(plane_peers))
-    idx_copies = []
-    for x, peer in z_peers:
-        for w in range(2):
-            copy = pltpu.make_async_remote_copy(
+
+    def idx_copies(x, peer):
+        return [
+            pltpu.make_async_remote_copy(
                 src_ref=idx_buf.at[0, w], dst_ref=idx_buf.at[x, w],
                 send_sem=idx_send_sem.at[x, w], recv_sem=idx_recv_sem.at[x, w],
                 device_id=peer, device_id_type=MESH,
             )
-            copy.start()
-            idx_copies.append(copy)
+            for w in range(2)
+        ]
+
+    def z_copy(x, peer):
+        return pltpu.make_async_remote_copy(
+            src_ref=z_send.at[x], dst_ref=z_recv.at[x],
+            send_sem=z_send_sem.at[x], recv_sem=z_recv_sem.at[x],
+            device_id=peer, device_id_type=MESH,
+        )
+
+    def u_copy():
+        return pltpu.make_async_remote_copy(
+            src_ref=u_send, dst_ref=u_recv, send_sem=u_sem.at[0], recv_sem=u_sem.at[1],
+            device_id=far_peer, device_id_type=MESH,
+        )
+
+    for x, peer in z_peers:
+
+        def send_indices(x=x, peer=peer):
+            for copy in idx_copies(x, peer):
+                copy.start()
+
+        unless_far(x, send_indices)
 
     for copy in gate_loads:
         copy.wait()
@@ -132,47 +167,63 @@
     h0, h1 = dot(t, right_gate[0]), dot(t, right_gate[1])
     u_ref[0] = h0[:width] - h1[width:]
     u_ref[1] = h0[width:] + h1[:width]
-    mix = jnp.concatenate([mix_rows[0], mix_rows[1]], axis=0)
-
-    def amplitudes(j, low, right, write):
-        at = pl.ds(pl.multiple_of(j * low_width, low_width), low_width)
-        u = jnp.concatenate([u_ref[0, at, :], u_ref[1, at, :]], axis=0).astype(jnp.bfloat16)
-        index_rows, lanes = low.shape
+
+    @pl.when(far)
+    def _():
+        u_send[...] = u_ref[:, far_rows, :].astype(u_send.dtype)
+        u_copy().start()
+
+    def amplitudes(mix_of, u, slot, write):
+        mix = jnp.concatenate([mix_of[0], mix_of[1]], axis=0)
+        index_rows, lanes = idx_buf.shape[2:]
         part = 2 if index_rows % 2 == 0 else 1
         for k in range(0, index_rows, part):
-            x = dot(mix, onehot(low[k : k + part], width))
-            v = dot(u, onehot(right[k : k + part], width))
+            x = dot(mix, onehot(idx_buf[slot, 0, k : k + part], width))
+            v = dot(u, onehot(idx_buf[slot, 1, k : k + part], width))
             x0, x1, v0, v1 = x[:low_width], x[low_width:], v[:low_width], v[low_width:]
             real = jnp.sum(x0 * v0 - x1 * v1, axis=0, keepdims=True)
             imag = jnp.sum(x0 * v1 + x1 * v0, axis=0, keepdims=True)
             write(pl.ds(k * lanes, part * lanes), jnp.concatenate([real, imag], axis=0))
 
+    def u_of(j):
+        at = pl.ds(pl.multiple_of(j * low_width, low_width), low_width)
+        return jnp.concatenate([u_ref[0, at, :], u_ref[1, at, :]], axis=0).astype(jnp.bfloat16)
+
     def write_own(at, value):
         own_ref[:, at] = value
 
-    amplitudes(me, idx_buf[0, 0], idx_buf[0, 1], write_own)
-
-    z_copies = []
-    for n, (x, peer) in enumerate(z_peers):
-        idx_copies[2 * n].wait_recv()
-        idx_copies[2 * n + 1].wait_recv()
-
-        def write_send(at, value, x=x):
-            z_send[x, :, at] = value.astype(z_send.dtype)
-
-        amplitudes(peer["bits"], idx_buf[x, 0], idx_buf[x, 1], write_send)
-        copy = pltpu.make_async_remote_copy(
-            src_ref=z_send.at[x], dst_ref=z_recv.at[x],
-            send_sem=z_send_sem.at[x], recv_sem=z_recv_sem.at[x],
-            device_id=peer, device_id_type=MESH,
-        )
-        copy.start()
-        z_copies.append(copy)
-
+    def add_own(at, value):
+        own_ref[:, at] += value
+
+    amplitudes(mix_rows, u_of(me), 0, write_own)
+
+    for x, peer in z_peers:
+
+        def send_partial(x=x, peer=peer):
+            def write_send(at, value):
+                z_send[x, :, at] = value.astype(z_send.dtype)
+
+            for copy in idx_copies(x, peer):
+                copy.wait_recv()
+            amplitudes(mix_rows, u_of(peer["bits"]), x, write_send)
+            z_copy(x, peer).start()
+
+        unless_far(x, send_partial)
+
+    @pl.when(far)
+    def _():
+        u_copy().wait_recv()
+        u = jnp.concatenate([u_recv[0], u_recv[1]], axis=0)
+        amplitudes(mix_far, u, 0, add_own)
+
+    for x, peer in z_peers:
+
+        def add_partial(x=x, peer=peer):
+            z_copy(x, peer).wait_recv()
+            own_ref[...] += z_recv[x].astype(jnp.float32)
+
+        unless_far(x, add_partial)
     own = own_ref[...]
-    for x in range(1, groups):
-        z_copies[x - 1].wait_recv()
-        own = own + z_recv[x].astype(jnp.float32)
     here = sec * reps + rep
     plane[here] = own.astype(plane.dtype)
     p_copies = []
@@ -190,7 +241,19 @@
     for n in range(1, sections * reps):
         result = result + plane[n].astype(jnp.float32)
     out_ref[...] = result * norm
-    for copy in idx_copies + z_copies + p_copies:
+    for x, peer in z_peers:
+
+        def finish(x=x, peer=peer):
+            for copy in idx_copies(x, peer) + [z_copy(x, peer)]:
+                copy.wait_send()
+
+        unless_far(x, finish)
+
+    @pl.when(far)
+    def _():
+        u_copy().wait_send()
+
+    for copy in p_copies:
         copy.wait_send()
 
 
@@ -219,19 +282,23 @@
             pltpu.VMEM((2, width // groups, width), bf16),
             pltpu.VMEM((2, width, width), bf16),
             pltpu.VMEM((2, width, width), f32),
+            pltpu.VMEM((2, width // groups, width), bf16),
+            pltpu.VMEM((2, width // groups, width), bf16),
+            pltpu.VMEM((2, width // groups, width), bf16),
             pltpu.VMEM((groups, 2) + index_shape, jnp.int32),
             pltpu.VMEM((2, count), f32),
             pltpu.VMEM((groups, 2, count), bf16),
             pltpu.VMEM((groups, 2, count), bf16),
             pltpu.VMEM((sections * reps, 2, count), bf16),
             dma((2, CHUNKS)),
-            dma((3,)),
+            dma((4,)),
             dma((groups, 2)),
             dma((groups, 2)),
             dma((groups,)),
             dma((groups,)),
             dma((sections * reps,)),
             dma((sections * reps,)),
+            dma((2,)),
         ],
         compiler_params=pltpu.CompilerParams(
             collective_id=0, has_side_effects=True, vmem_limit_bytes=16 * 1024 * 1024

time: 18 us -> 18 us (level)
  no operation moved by 1% of the time
where the time goes in v3:
time: 18 us; the launch traced here: 17.8 us
  Pallas kernels  17.2 us (96%)
  local copies, waits for them, and re-layouts  0.6 us (3%)
    pallas_call x1, Pallas kernels, body(): pl.pallas_call(functools.partial(kernel, sizes, norm), out_shape=jax.Shap...  17.2 us
    unnamed x1, local copies, waits for them, and re-layouts  0.6 us

profile of v3, /device:TPU:0, one launch (start us, length us, event | category | flops | bytes accessed | tf_op | source)
XLA Modules:
  0.0 17.8 jit_solution(4385121645839083701)
XLA Ops:
  0.0 17.2 %amplitudes.1 = f32[2,1024]{1,0:T(2,128)S(1)} custom-call(bf16[1024,2,256]{2,1,0:T(2,128)(2,1)} %bitcast.4, bf16[1024,2,256]{2,1,0:T(2,128)(2,1)} %bitcast.5, bf16[2,256,256]{2,1,0:T(8,128)(2,1)} %left_gate_hbm.1, bf16[2,256,256]{2,1,0:T(8,128)(2,1)} %mix_hbm.1, bf16[2,256,256]{2,1,0:T(8,128)(2,1)} %right_gate_hbm.1, s32[8,128]{1,0:T(8,128)} %bitcast.6, ...), custom_call_target="tpu_custom_call" | custom-call | tf_op jit(solution)/shard_map/amplitudes/pallas_call | solution.py:273
  17.2 0.6 %copy.9 = f32[2,1024]{1,0:T(2,128)} copy(f32[2,1024]{1,0:T(2,128)S(1)} %amplitudes.1) | data formatting | bytes 16384

commit v4 on v2

--- a/solution.py
+++ b/solution.py
@@ -44,25 +44,27 @@
     left_hbm, right_hbm, left_gate_hbm, mix_hbm, right_gate_hbm, low_hbm, right_index_hbm,
     out_ref,
     left_buf, right_buf, left_gate, mix_rows, right_gate, u_ref,
-    idx_buf, own_ref, z_send, z_recv, plane,
-    load_sem, gate_sem, idx_send_sem, idx_recv_sem, z_send_sem, z_recv_sem, p_send_sem, p_recv_sem,
+    idx_buf, own_ref, z_send, z_recv, pair_buf, plane,
+    load_sem, gate_sem, idx_send_sem, idx_recv_sem, z_send_sem, z_recv_sem, p_send_sem, p_recv_sem, pair_sem,
 ):
     groups, sections, reps = sizes
     me, sec, rep = lax.axis_index("bits"), lax.axis_index("section"), lax.axis_index("rep")
     width = left_gate.shape[1]
     low_width = width // groups
     z_peers = [(x, {"bits": flip(me, x, groups)}) for x in range(1, groups)]
+    halves = reps // 2
+    pair_peer = {"rep": flip(rep, 1, reps)}
     plane_peers = []
     for a in reversed(range(sections)):
-        for b in reversed(range(reps)):
+        for b in reversed(range(halves)):
             if a or b:
-                s, r = flip(sec, a, sections), flip(rep, b, reps)
-                plane_peers.append((s * reps + r, {"section": s, "rep": r}, a * reps + b))
+                there = {"section": flip(sec, a, sections), "rep": flip(rep, 2 * b, reps)}
+                plane_peers.append((there, a * halves + b))
 
     barrier = pltpu.get_barrier_semaphore()
     for _, peer in z_peers:
         pl.semaphore_signal(barrier, inc=1, device_id=peer, device_id_type=MESH)
-    for _, peer, _ in plane_peers:
+    for peer in [pair_peer] + [peer for peer, _ in plane_peers]:
         pl.semaphore_signal(barrier, inc=1, device_id=peer, device_id_type=MESH)
 
     rows = left_buf.shape[0]
@@ -111,7 +113,7 @@
 
     for copy in idx_loads:
         copy.wait()
-    pl.semaphore_wait(barrier, len(z_peers) + len(plane_peers))
+    pl.semaphore_wait(barrier, len(z_peers) + 1 + len(plane_peers))
     idx_copies = []
     for x, peer in z_peers:
         for w in range(2):
@@ -173,10 +175,19 @@
     for x in range(1, groups):
         z_copies[x - 1].wait_recv()
         own = own + z_recv[x].astype(jnp.float32)
-    here = sec * reps + rep
-    plane[here] = own.astype(plane.dtype)
+    side = lax.rem(rep, 2)
+    pair_buf[side] = own.astype(pair_buf.dtype)
+    pair_copy = pltpu.make_async_remote_copy(
+        src_ref=pair_buf.at[side], dst_ref=pair_buf.at[side],
+        send_sem=pair_sem.at[0], recv_sem=pair_sem.at[1],
+        device_id=pair_peer, device_id_type=MESH,
+    )
+    pair_copy.start()
+    pair_copy.wait_recv()
+    here = sec * halves + rep // 2
+    plane[here] = (pair_buf[0].astype(jnp.float32) + pair_buf[1].astype(jnp.float32)).astype(plane.dtype)
     p_copies = []
-    for there, peer, n in plane_peers:
+    for peer, n in plane_peers:
         copy = pltpu.make_async_remote_copy(
             src_ref=plane.at[here], dst_ref=plane.at[here],
             send_sem=p_send_sem.at[n], recv_sem=p_recv_sem.at[n],
@@ -187,10 +198,10 @@
     for copy in p_copies:
         copy.wait_recv()
     result = plane[0].astype(jnp.float32)
-    for n in range(1, sections * reps):
+    for n in range(1, sections * halves):
         result = result + plane[n].astype(jnp.float32)
     out_ref[...] = result * norm
-    for copy in idx_copies + z_copies + p_copies:
+    for copy in idx_copies + z_copies + [pair_copy] + p_copies:
         copy.wait_send()
 
 
@@ -223,15 +234,17 @@
             pltpu.VMEM((2, count), f32),
             pltpu.VMEM((groups, 2, count), bf16),
             pltpu.VMEM((groups, 2, count), bf16),
-            pltpu.VMEM((sections * reps, 2, count), bf16),
+            pltpu.VMEM((2, 2, count), bf16),
+            pltpu.VMEM((sections * reps // 2, 2, count), bf16),
             dma((2, CHUNKS)),
             dma((3,)),
             dma((groups, 2)),
             dma((groups, 2)),
             dma((groups,)),
             dma((groups,)),
-            dma((sections * reps,)),
-            dma((sections * reps,)),
+            dma((sections * reps // 2,)),
+            dma((sections * reps // 2,)),
+            dma((2,)),
         ],
         compiler_params=pltpu.CompilerParams(
             collective_id=0, has_side_effects=True, vmem_limit_bytes=16 * 1024 * 1024

time: 18 us -> 17.9 us (level)
  no operation moved by 1% of the time
where the time goes in v4:
time: 17.9 us; the launch traced here: 17.7 us
  Pallas kernels  17.1 us (96%)
  local copies, waits for them, and re-layouts  0.6 us (3%)
    pallas_call x1, Pallas kernels, body(): pl.pallas_call(functools.partial(kernel, sizes, norm), out_shape=jax.Shap...  17.1 us
    unnamed x1, local copies, waits for them, and re-layouts  0.6 us

profile of v4, /device:TPU:0, one launch (start us, length us, event | category | flops | bytes accessed | tf_op | source)
XLA Modules:
  0.0 17.7 jit_solution(13391302109335536991)
XLA Ops:
  0.0 17.1 %amplitudes.1 = f32[2,1024]{1,0:T(2,128)S(1)} custom-call(bf16[1024,2,256]{2,1,0:T(2,128)(2,1)} %bitcast.4, bf16[1024,2,256]{2,1,0:T(2,128)(2,1)} %bitcast.5, bf16[2,256,256]{2,1,0:T(8,128)(2,1)} %left_gate_hbm.1, bf16[2,256,256]{2,1,0:T(8,128)(2,1)} %mix_hbm.1, bf16[2,256,256]{2,1,0:T(8,128)(2,1)} %right_gate_hbm.1, s32[8,128]{1,0:T(8,128)} %bitcast.6, ...), custom_call_target="tpu_custom_call" | custom-call | tf_op jit(solution)/shard_map/amplitudes/pallas_call | solution.py:221
  17.1 0.6 %copy.9 = f32[2,1024]{1,0:T(2,128)} copy(f32[2,1024]{1,0:T(2,128)S(1)} %amplitudes.1) | data formatting | bytes 16384

commit v5 on v2

--- a/solution.py
+++ b/solution.py
@@ -44,7 +44,7 @@
     left_hbm, right_hbm, left_gate_hbm, mix_hbm, right_gate_hbm, low_hbm, right_index_hbm,
     out_ref,
     left_buf, right_buf, left_gate, mix_rows, right_gate, u_ref,
-    idx_buf, own_ref, z_send, z_recv, plane,
+    idx_own, idx_buf, own_ref, z_send, z_recv, plane,
     load_sem, gate_sem, idx_send_sem, idx_recv_sem, z_send_sem, z_recv_sem, p_send_sem, p_recv_sem,
 ):
     groups, sections, reps = sizes
@@ -85,11 +85,15 @@
         pltpu.make_async_copy(mix_hbm.at[:, mine, :], mix_rows, gate_sem.at[2]),
     ]
     idx_loads = [
-        pltpu.make_async_copy(low_hbm, idx_buf.at[0, 0], idx_recv_sem.at[0, 0]),
-        pltpu.make_async_copy(right_index_hbm, idx_buf.at[0, 1], idx_recv_sem.at[0, 1]),
+        pltpu.make_async_copy(low_hbm, idx_own.at[0], gate_sem.at[3]),
+        pltpu.make_async_copy(right_index_hbm, idx_own.at[1], gate_sem.at[4]),
     ]
     for copy in idx_loads + gate_loads:
         copy.start()
+
+    for copy in idx_loads:
+        copy.wait()
+    idx_buf[0] = idx_own[...].astype(jnp.float32).astype(idx_buf.dtype)
 
     block = min(width, step)
     row_at = lax.broadcasted_iota(jnp.int32, (block, block), 0)
@@ -109,19 +113,16 @@
         total = total + dot_t(left_buf[pl.ds(c * step, step), :], jnp.concatenate(pieces, axis=0))
     q = total.astype(jnp.bfloat16)
 
-    for copy in idx_loads:
-        copy.wait()
     pl.semaphore_wait(barrier, len(z_peers) + len(plane_peers))
     idx_copies = []
     for x, peer in z_peers:
-        for w in range(2):
-            copy = pltpu.make_async_remote_copy(
-                src_ref=idx_buf.at[0, w], dst_ref=idx_buf.at[x, w],
-                send_sem=idx_send_sem.at[x, w], recv_sem=idx_recv_sem.at[x, w],
-                device_id=peer, device_id_type=MESH,
-            )
-            copy.start()
-            idx_copies.append(copy)
+        copy = pltpu.make_async_remote_copy(
+            src_ref=idx_buf.at[0], dst_ref=idx_buf.at[x],
+            send_sem=idx_send_sem.at[x], recv_sem=idx_recv_sem.at[x],
+            device_id=peer, device_id_type=MESH,
+        )
+        copy.start()
+        idx_copies.append(copy)
 
     for copy in gate_loads:
         copy.wait()
@@ -150,17 +151,17 @@
     def write_own(at, value):
         own_ref[:, at] = value
 
-    amplitudes(me, idx_buf[0, 0], idx_buf[0, 1], write_own)
+    amplitudes(me, idx_own[0], idx_own[1], write_own)
 
     z_copies = []
     for n, (x, peer) in enumerate(z_peers):
-        idx_copies[2 * n].wait_recv()
-        idx_copies[2 * n + 1].wait_recv()
+        idx_copies[n].wait_recv()
+        low, right = idx_buf[x].astype(jnp.float32).astype(jnp.int32)
 
         def write_send(at, value, x=x):
             z_send[x, :, at] = value.astype(z_send.dtype)
 
-        amplitudes(peer["bits"], idx_buf[x, 0], idx_buf[x, 1], write_send)
+        amplitudes(peer["bits"], low, right, write_send)
         copy = pltpu.make_async_remote_copy(
             src_ref=z_send.at[x], dst_ref=z_recv.at[x],
             send_sem=z_send_sem.at[x], recv_sem=z_recv_sem.at[x],
@@ -219,15 +220,16 @@
             pltpu.VMEM((2, width // groups, width), bf16),
             pltpu.VMEM((2, width, width), bf16),
             pltpu.VMEM((2, width, width), f32),
-            pltpu.VMEM((groups, 2) + index_shape, jnp.int32),
+            pltpu.VMEM((2,) + index_shape, jnp.int32),
+            pltpu.VMEM((groups, 2) + index_shape, bf16),
             pltpu.VMEM((2, count), f32),
             pltpu.VMEM((groups, 2, count), bf16),
             pltpu.VMEM((groups, 2, count), bf16),
             pltpu.VMEM((sections * reps, 2, count), bf16),
             dma((2, CHUNKS)),
-            dma((3,)),
-            dma((groups, 2)),
-            dma((groups, 2)),
+            dma((5,)),
+            dma((groups,)),
+            dma((groups,)),
             dma((groups,)),
             dma((groups,)),
             dma((sections * reps,)),

time: 18 us -> 18.1 us (level)
  no operation moved by 1% of the time
where the time goes in v5:
time: 18.1 us; the launch traced here: 17.9 us
  Pallas kernels  17.3 us (96%)
  local copies, waits for them, and re-layouts  0.6 us (3%)
    pallas_call x1, Pallas kernels, body(): pl.pallas_call(functools.partial(kernel, sizes, norm), out_shape=jax.Shap...  17.3 us
    unnamed x1, local copies, waits for them, and re-layouts  0.6 us

profile of v5, /device:TPU:0, one launch (start us, length us, event | category | flops | bytes accessed | tf_op | source)
XLA Modules:
  0.0 17.9 jit_solution(13105062963683893979)
XLA Ops:
  0.0 17.3 %amplitudes.1 = f32[2,1024]{1,0:T(2,128)S(1)} custom-call(bf16[1024,2,256]{2,1,0:T(2,128)(2,1)} %bitcast.4, bf16[1024,2,256]{2,1,0:T(2,128)(2,1)} %bitcast.5, bf16[2,256,256]{2,1,0:T(8,128)(2,1)} %left_gate_hbm.1, bf16[2,256,256]{2,1,0:T(8,128)(2,1)} %mix_hbm.1, bf16[2,256,256]{2,1,0:T(8,128)(2,1)} %right_gate_hbm.1, s32[8,128]{1,0:T(8,128)} %bitcast.6, ...), custom_call_target="tpu_custom_call" | custom-call | tf_op jit(solution)/shard_map/amplitudes/pallas_call | solution.py:211
  17.3 0.6 %copy.9 = f32[2,1024]{1,0:T(2,128)} copy(f32[2,1024]{1,0:T(2,128)S(1)} %amplitudes.1) | data formatting | bytes 16384

commit v6 on v2

--- a/solution.py
+++ b/solution.py
@@ -91,6 +91,20 @@
     for copy in idx_loads + gate_loads:
         copy.start()
 
+    for copy in idx_loads:
+        copy.wait()
+    pl.semaphore_wait(barrier, len(z_peers) + len(plane_peers))
+    idx_copies = []
+    for x, peer in z_peers:
+        for w in range(2):
+            copy = pltpu.make_async_remote_copy(
+                src_ref=idx_buf.at[0, w], dst_ref=idx_buf.at[x, w],
+                send_sem=idx_send_sem.at[x, w], recv_sem=idx_recv_sem.at[x, w],
+                device_id=peer, device_id_type=MESH,
+            )
+            copy.start()
+            idx_copies.append(copy)
+
     block = min(width, step)
     row_at = lax.broadcasted_iota(jnp.int32, (block, block), 0)
     column_at = lax.broadcasted_iota(jnp.int32, (block, block), 1)
@@ -108,20 +122,6 @@
             pieces.append(jnp.concatenate([r * sign, dot(swap, r).astype(jnp.bfloat16)], axis=1))
         total = total + dot_t(left_buf[pl.ds(c * step, step), :], jnp.concatenate(pieces, axis=0))
     q = total.astype(jnp.bfloat16)
-
-    for copy in idx_loads:
-        copy.wait()
-    pl.semaphore_wait(barrier, len(z_peers) + len(plane_peers))
-    idx_copies = []
-    for x, peer in z_peers:
-        for w in range(2):
-            copy = pltpu.make_async_remote_copy(
-                src_ref=idx_buf.at[0, w], dst_ref=idx_buf.at[x, w],
-                send_sem=idx_send_sem.at[x, w], recv_sem=idx_recv_sem.at[x, w],
-                device_id=peer, device_id_type=MESH,
-            )
-            copy.start()
-            idx_copies.append(copy)
 
     for copy in gate_loads:
         copy.wait()

time: 18 us -> 18 us (level)
  no operation moved by 1% of the time
where the time goes in v6:
time: 18 us; the launch traced here: 17.8 us
  Pallas kernels  17.2 us (96%)
  local copies, waits for them, and re-layouts  0.6 us (3%)
    pallas_call x1, Pallas kernels, body(): pl.pallas_call(functools.partial(kernel, sizes, norm), out_shape=jax.Shap...  17.2 us
    unnamed x1, local copies, waits for them, and re-layouts  0.6 us

profile of v6, /device:TPU:0, one launch (start us, length us, event | category | flops | bytes accessed | tf_op | source)
XLA Modules:
  0.0 17.8 jit_solution(3713301445884959964)
XLA Ops:
  0.0 17.2 %amplitudes.1 = f32[2,1024]{1,0:T(2,128)S(1)} custom-call(bf16[1024,2,256]{2,1,0:T(2,128)(2,1)} %bitcast.4, bf16[1024,2,256]{2,1,0:T(2,128)(2,1)} %bitcast.5, bf16[2,256,256]{2,1,0:T(8,128)(2,1)} %left_gate_hbm.1, bf16[2,256,256]{2,1,0:T(8,128)(2,1)} %mix_hbm.1, bf16[2,256,256]{2,1,0:T(8,128)(2,1)} %right_gate_hbm.1, s32[8,128]{1,0:T(8,128)} %bitcast.6, ...), custom_call_target="tpu_custom_call" | custom-call | tf_op jit(solution)/shard_map/amplitudes/pallas_call | solution.py:210
  17.2 0.6 %copy.9 = f32[2,1024]{1,0:T(2,128)} copy(f32[2,1024]{1,0:T(2,128)S(1)} %amplitudes.1) | data formatting | bytes 16384
